TPU v7x, 32 devices: a whole 2x2x4 slice. The times are simulated.
32 devices in a mesh: band: 2 (over y), row: 16 (over z, x, core).
Axes of the slice: x: 2, y: 2, z: 4, core: 2. Of those that a mesh axis runs over, the one named last changes fastest.
Arguments:
- coeffs: bfloat16 [2, 6144, 4096], P(None, 'row', 'band'), may hold values from -6 to 6
- rotation: bfloat16 [2, 4096, 4096], P(None, 'row', 'band'), may hold values from -0.0625 to 0.0625
Outputs:
- rotated: bfloat16 [2, 6144, 4096], P(None, 'row', 'band')
All inputs are finite; a program needn't handle non-finite values.
Results may differ from a plain program's by a relative error of at most 0.0014.
Values may be sent and summed in bfloat16 or wider, within the bound.
A program may use at most 128 MiB of HBM per device.

v0:
```python
import functools

import jax
import jax.numpy as jnp
from jax import lax
from jax.experimental import pallas as pl
from jax.experimental.pallas import tpu as pltpu
from jax.sharding import PartitionSpec as P

MESH = pl.DeviceIdType.MESH
CORES = 2
PIECE_BYTES = 256 * 1024


def kernel(chips, bands, cuts, tile, coeffs_ref, rotation_ref, out_ref, held, whole, total,
           ring_send, ring_recv, pair_send, pair_recv, band_send, band_recv, own_sem):
    band = lax.axis_index("band")
    row = lax.axis_index("row")
    depth = rotation_ref.shape[1]
    columns = rotation_ref.shape[2] // cuts
    width = coeffs_ref.shape[2]
    half = chips // 2

    chip = row // CORES
    core = row % CORES
    line = chip // 2
    side = chip % 2
    place = line + side * (chips - 1 - 2 * line)

    def chip_at(position):
        back = position // half
        return (1 - back) * 2 * position + back * (2 * (chips - 1 - position) + 1)

    ahead = chip_at((place + 1) % chips) * CORES + core
    behind = chip_at((place + chips - 1) % chips) * CORES + core
    sibling = chip * CORES + (1 - core)
    partners = [(band + step) % bands for step in range(1, bands)]

    barrier = pltpu.get_barrier_semaphore()
    for other in (ahead, behind, sibling):
        pl.semaphore_signal(barrier, inc=1, device_id={"row": other}, device_id_type=MESH)
    for other in partners:
        pl.semaphore_signal(barrier, inc=1, device_id={"band": other}, device_id_type=MESH)
    pl.semaphore_wait(barrier, 3 + len(partners))

    def mine(part, step, piece):
        return held.at[part, step, piece, pl.ds(pl.multiple_of(core * depth, depth), depth)]

    def source(part, step, piece):
        if step == 0:
            return rotation_ref.at[part, :, pl.ds(piece * columns, columns)]
        return mine(part, step, piece)

    def hop(part, step, piece):
        return pltpu.make_async_remote_copy(
            src_ref=source(part, step, piece),
            dst_ref=mine(part, step + 1, piece),
            send_sem=ring_send.at[part, step, piece],
            recv_sem=ring_recv.at[part, step, piece],
            device_id={"row": (ahead, behind)[part]},
            device_id_type=MESH,
        )

    def share(part, step, piece):
        return pltpu.make_async_remote_copy(
            src_ref=source(part, step, piece),
            dst_ref=mine(part, step, piece),
            send_sem=pair_send.at[part, step, piece],
            recv_sem=pair_recv.at[part, step, piece],
            device_id={"row": sibling},
            device_id_type=MESH,
        )

    pieces = [(part, piece) for piece in range(cuts) for part in range(2)]
    for part, piece in pieces:
        hop(part, 0, piece).start()
    spread = [
        pltpu.make_async_remote_copy(
            src_ref=coeffs_ref,
            dst_ref=whole.at[band],
            send_sem=band_send.at[i],
            recv_sem=band_recv.at[i],
            device_id={"band": other},
            device_id_type=MESH,
        )
        for i, other in enumerate(partners)
    ]
    for copy in spread:
        copy.start()
    for part, piece in pieces:
        share(part, 0, piece).start()
    own = [pltpu.make_async_copy(coeffs_ref, whole.at[band], own_sem.at[0])]
    for i, (part, piece) in enumerate(pieces):
        own.append(pltpu.make_async_copy(source(part, 0, piece), mine(part, 0, piece), own_sem.at[1 + i]))
    for copy in own:
        copy.start()
    for copy in own:
        copy.wait()

    def multiply(step, piece):
        for part in range(2):
            share(part, step, piece).wait_recv()
        spans = []
        for origin in ((place + chips - step) % chips, (place + step) % chips):
            first = chip_at(origin) * (CORES * depth)
            spans.append((first // width, pl.multiple_of(first % width, CORES * depth)))

        def left(part, span):
            return whole[span[0], part, :, pl.ds(span[1], CORES * depth)]

        @pl.loop(0, columns // tile)
        def _(i):
            cut = pl.ds(pl.multiple_of(i * tile, tile), tile)
            out = pl.ds(pl.multiple_of(piece * columns + i * tile, tile), tile)
            real = held[0, step, piece, :, cut]
            imag = held[1, step, piece, :, cut]
            dot = functools.partial(jnp.dot, preferred_element_type=jnp.float32)
            real_term = dot(left(0, spans[0]), real) - dot(left(1, spans[1]), imag)
            if step > 0:
                real_term += total[0, :, out]
            imag_term = dot(left(1, spans[0]), real) + dot(left(0, spans[1]), imag)
            if step > 0:
                imag_term += total[1, :, out]
            if step < chips - 1:
                total[0, :, out] = real_term
                total[1, :, out] = imag_term
            else:
                out_ref[0, :, out] = real_term.astype(out_ref.dtype)
                out_ref[1, :, out] = imag_term.astype(out_ref.dtype)

    units = [(step, piece) for step in range(chips) for piece in range(cuts)]
    events = (chips - 1) * cuts
    begin = events // 2
    done = 0
    for event in range(events):
        step, piece = 1 + event // cuts, event % cuts
        for part in range(2):
            hop(part, step - 1, piece).wait_recv()
            if step < chips - 1:
                hop(part, step, piece).start()
            share(part, step, piece).start()
        if event == begin:
            for copy in spread:
                copy.wait_recv()
        if event >= begin:
            goal = min(event + cuts, 3 * (event - begin + 1))
            for unit in units[done:goal]:
                multiply(*unit)
            done = max(done, goal)
    for unit in units[done:]:
        multiply(*unit)

    for copy in spread:
        copy.wait_send()
    for step in range(chips):
        for part, piece in pieces:
            if step < chips - 1:
                hop(part, step, piece).wait_send()
            share(part, step, piece).wait_send()


def solution(mesh):
    bands, rows = mesh.shape["band"], mesh.shape["row"]
    chips = rows // CORES

    def body(coeffs, rotation):
        depth, columns = rotation.shape[1:]
        cuts = max(1, min(4, depth * columns * 2 // PIECE_BYTES))
        tile = min(256, columns // cuts)
        return pl.pallas_call(
            functools.partial(kernel, chips, bands, cuts, tile),
            out_shape=pltpu.VMEM(coeffs.shape, jnp.bfloat16),
            in_specs=[pl.BlockSpec(memory_space=pl.ANY)] * 2,
            out_specs=pl.BlockSpec(memory_space=pltpu.VMEM),
            scratch_shapes=[
                pltpu.VMEM((2, chips, cuts, CORES * depth, columns // cuts), jnp.bfloat16),
                pltpu.VMEM((bands,) + coeffs.shape, jnp.bfloat16),
                pltpu.VMEM(coeffs.shape, jnp.float32),
                pltpu.SemaphoreType.DMA((2, chips - 1, cuts)),
                pltpu.SemaphoreType.DMA((2, chips - 1, cuts)),
                pltpu.SemaphoreType.DMA((2, chips, cuts)),
                pltpu.SemaphoreType.DMA((2, chips, cuts)),
                pltpu.SemaphoreType.DMA((bands - 1,)),
                pltpu.SemaphoreType.DMA((bands - 1,)),
                pltpu.SemaphoreType.DMA((1 + 2 * cuts,)),
            ],
            compiler_params=pltpu.CompilerParams(
                collective_id=0, has_side_effects=True, vmem_limit_bytes=54 * 1024 * 1024
            ),
        )(coeffs, rotation)

    in_specs = (P(None, "row", "band"), P(None, "row", "band"))
    out_specs = P(None, "row", "band")
    return jax.shard_map(body, mesh=mesh, in_specs=in_specs, out_specs=out_specs, check_vma=False)
```

profile of v0, /device:TPU:25, one launch (start us, length us, event | category | flops | bytes accessed | tf_op | source)
XLA Modules:
  0.0 167.9 jit_solution(13264953546038983685)
XLA Ops:
  0.0 166.2 %shard_map.28 = bf16[2,384,2048]{2,1,0:T(8,128)(2,1)S(1)} custom-call(bf16[2,384,2048]{2,1,0:T(8,128)(2,1)} %coeffs_ref.1, bf16[2,256,2048]{2,1,0:T(8,128)(2,1)} %rotation_ref.1), custom_call_target="tpu_custom_call" | custom-call | tf_op jit(solution)/shard_map/pallas_call | solution.py:170
  166.2 1.7 copy.4
where the time goes:
time: 169 us; the launch traced here: 168 us
  Pallas kernels  166 us (98%)
    pallas_call x1, Pallas kernels, body(): pl.pallas_call(functools.partial(kernel, chips, bands, cuts, tile), out_s...  166 us

commit v1 on v0

v1 whole, which is shorter than its diff:
```python
import functools

import jax
import jax.numpy as jnp
from jax import lax
from jax.experimental import pallas as pl
from jax.experimental.pallas import tpu as pltpu
from jax.sharding import PartitionSpec as P

MESH = pl.DeviceIdType.MESH
CORES = 2
SIDES = 2
CHUNK = 512
LANES = 128
TILE = 256
FORWARDS = (2, 4, 5, 8)


def kernel(lines, bands, cuts, chunk, coeffs_ref, rotation_ref, out_ref, held, whole, total, extra, staged,
           own_sem, cross_send, cross_recv, line_send, relay_send, line_recv, mate_send, mate_recv,
           pair_send, pair_recv, side_send, side_recv, band_send, band_recv, pass_send, pass_recv,
           out_send, out_recv):
    band = lax.axis_index("band")
    row = lax.axis_index("row")
    depth = rotation_ref.shape[1]
    width = coeffs_ref.shape[2]
    share = rotation_ref.shape[2] // SIDES
    layer = SIDES * CORES * depth
    pieces = len(cuts)
    last = pieces - 1
    chunks = width // chunk
    early = chunks // 2 if bands == 2 else 0
    hops = lines - 1

    line = row // (SIDES * CORES)
    side = (row // CORES) % SIDES
    core = row % CORES

    def at(z, x, c):
        return {"row": (z * SIDES + x) * CORES + c}

    flank = at(line, 1 - side, core)
    sibling = at(line, side, 1 - core)
    partners = [{"band": (band + step) % bands} for step in range(1, bands)]
    above = line < lines - 1
    below = line > 0
    ways = ((above, at(line + 1, side, core)), (below, at(line - 1, side, core)))

    near = jnp.minimum(line, lines - 1 - line)
    rise = jnp.where(2 * line < lines - 1, 1, -1)
    others = []
    for i in range(1, lines):
        step = jnp.where(i <= 2 * near, ((i + 1) // 2) * (1 if i % 2 else -1), rise * (i - near))
        other = line + step
        onward = jnp.where(step > 0, -1, 1)
        valid = jnp.logical_and(line + onward >= 0, line + onward < lines)
        target = jnp.where(valid, line + onward, line - onward)
        others.append((other, valid, at(target, side, core)))

    barrier = pltpu.get_barrier_semaphore()
    for other in [flank, sibling] + partners:
        pl.semaphore_signal(barrier, inc=1, device_id=other, device_id_type=MESH)
    for exists, other in ways:
        @pl.when(exists)
        def _(other=other):
            pl.semaphore_signal(barrier, inc=1, device_id=other, device_id_type=MESH)
    pl.semaphore_wait(barrier, 2 + len(partners) + jnp.where(above, 1, 0) + jnp.where(below, 1, 0))

    def remote(source, target, send, recv, device):
        return pltpu.make_async_remote_copy(
            src_ref=source, dst_ref=target, send_sem=send, recv_sem=recv, device_id=device, device_id_type=MESH
        )

    def rows(z, x, c):
        return pl.ds(pl.multiple_of(((z * SIDES + x) * CORES + c) * depth, depth), depth)

    def cols(s):
        return pl.ds(cuts[s][0], cuts[s][1])

    def quarter(x, s):
        return pl.ds(pl.multiple_of(x * share + cuts[s][0], LANES), cuts[s][1])

    def half(x):
        return pl.ds(pl.multiple_of(x * share, LANES), share)

    def block(s, z, rel):
        return held.at[:, rows(z, (side, 1 - side)[rel], core), cols(s)]

    def cross(s):
        return remote(rotation_ref.at[:, :, quarter(1 - side, s)], block(s, line, 0), cross_send.at[s], cross_recv.at[s], flank)

    def lift(s, rel, way):
        source = block(s, line, 1) if rel else rotation_ref.at[:, :, quarter(side, s)]
        return remote(source, block(s, line, rel), line_send.at[s, rel, way], line_recv.at[s, line, rel], ways[way][1])

    def relay(s, i, rel):
        piece = block(s, others[i][0], rel)
        return remote(piece, piece, relay_send.at[s, i, rel], line_recv.at[s, others[i][0], rel], others[i][2])

    def give(s, z, rel):
        piece = block(s, z, rel)
        return remote(piece, piece, pair_send.at[s, z, rel], pair_recv.at[s, z, rel], sibling)

    def span(j):
        return pl.ds(j * chunk, chunk)

    def beside(j):
        return remote(coeffs_ref.at[:, :, span(j)], whole.at[side, band, :, :, span(j)], side_send.at[j], side_recv.at[j], flank)

    def spread(n, j):
        return remote(coeffs_ref.at[:, :, span(j)], whole.at[side, band, :, :, span(j)], band_send.at[n, j], band_recv.at[n, j], partners[n])

    def hand(n, j):
        piece = whole.at[1 - side, band, :, :, span(j)]
        return remote(piece, piece, pass_send.at[n, j], pass_recv.at[n, j], partners[n])

    def back(s):
        return remote(staged.at[:, :, cols(s)], out_ref.at[:, :, quarter(side, s)], out_send.at[s], out_recv.at[s], flank)

    mate = remote(rotation_ref.at[:, :, half(side)], held.at[:, rows(line, side, core), :], mate_send.at[0], mate_recv.at[0], sibling)
    own = [
        pltpu.make_async_copy(rotation_ref.at[:, :, half(side)], held.at[:, rows(line, side, core), :], own_sem.at[0]),
        pltpu.make_async_copy(coeffs_ref, whole.at[side, band], own_sem.at[1]),
    ]

    def start_own(s):
        for way, (exists, _) in enumerate(ways):
            @pl.when(exists)
            def _(way=way):
                lift(s, 0, way).start()

    crossed = 0
    passed = 0

    def feed(until):
        nonlocal crossed, passed
        for kind, index in order[crossed + passed:until]:
            if kind == 0:
                cross(index).start()
                crossed += 1
            else:
                beside(index).start()
                passed += 1

    order = [(0, 0)]
    for j in range(chunks):
        order.append((1, j))
        if j % 2 == 0 and j // 2 + 1 < pieces:
            order.append((0, j // 2 + 1))
    order += [(0, s) for s in range(pieces) if (0, s) not in order]

    start_own(0)
    feed(1)
    for j in range(early):
        for n in range(bands - 1):
            spread(n, j).start()
    feed(4)
    if pieces > 1:
        start_own(1)
    mate.start()
    for copy in own:
        copy.start()
    total[...] = jnp.zeros_like(total)

    def unit(x, start, size, target, to, s):
        which = start // width
        at_k = pl.ds(pl.multiple_of(start % width, LANES), size)
        deep = pl.ds(pl.multiple_of(start, LANES), size)
        real, imag = held[0, deep, cols(s)], held[1, deep, cols(s)]
        dot = functools.partial(jnp.dot, preferred_element_type=jnp.float32)
        left_real = whole[x, which, 0, :, at_k]
        left_imag = whole[x, which, 1, :, at_k]
        target[0, :, to] += dot(left_real, real) - dot(left_imag, imag)
        target[1, :, to] += dot(left_imag, real) + dot(left_real, imag)

    every = bands * chunks
    pair = 2 if chunks % 4 == 0 else 1

    def sweep(x, first, stop, target, to, s):
        @pl.loop(first // pair, stop // pair)
        def _(u):
            unit(x, ((band * chunks + u * pair) % every) * chunk, pair * chunk, target, to, s)

    ready = set()

    def once(key, waits):
        if key not in ready:
            ready.add(key)
            for wait in waits():
                wait()

    def have_mate():
        once("mate", lambda: [mate.wait_recv, own[0].wait])

    def have_own():
        once("own", lambda: [own[1].wait] + [spread(n, j).wait_recv for n in range(bands - 1) for j in range(early)])

    def have_layer(s, i):
        if i < 0:
            have_mate()
            once((s, i), lambda: [give(s, line, 1).wait_recv])
        else:
            once((s, i), lambda: [give(s, others[i][0], rel).wait_recv for rel in range(2)])

    def have_all(s):
        for i in range(-1, hops):
            have_layer(s, i)

    def have_side():
        once("pass", lambda: [hand(n, j).wait_recv for n in range(bands - 1) for j in range(chunks)])

    def have_late(j):
        once(("late", j), lambda: [spread(n, j).wait_recv for n in range(bands - 1)])

    pending = []

    def flush():
        while pending:
            back(pending.pop()).start()

    def settle(s):
        staged[:, :, cols(s)] = extra[:, :, pl.ds(0, cuts[s][1])].astype(staged.dtype)
        pending.append(s)

    def mine(s):
        have_own()
        have_all(s)
        sweep(side, 0, chunks + early, total, cols(s), s)

    def theirs(s):
        have_own()
        have_side()
        have_all(s)
        to = pl.ds(0, cuts[s][1])
        extra[:, :, to] = jnp.zeros((2, extra.shape[1], cuts[s][1]), extra.dtype)
        sweep(1 - side, 0, every, extra, to, s)
        settle(s)

    def partial(i):
        have_own()
        have_side()
        have_layer(last, i)
        z = line if i < 0 else others[i][0]
        to = pl.ds(0, cuts[last][1])
        if i < 0:
            extra[:, :, to] = jnp.zeros((2, extra.shape[1], cuts[last][1]), extra.dtype)
        unit(1 - side, z * layer, layer, extra, to, last)

    def late(j, s):
        for n in range(1, bands):
            if n > 1 or j >= early:
                unit(side, ((band + n) % bands) * width + j * chunk, chunk, total, cols(s), s)

    work = {}

    def plan(point, job):
        work.setdefault(min(point, pieces * hops), []).append(job)

    forwards = {}
    for j in range(chunks):
        hint = FORWARDS[j] if j < len(FORWARDS) else FORWARDS[-1]
        forwards.setdefault(min(hint, pieces * hops), []).append(j)
    begin = max(0, (pieces - 2) * hops + 1)
    for s in range(last):
        plan(max((s + 1) * hops + 1, begin + s), functools.partial(theirs, s))
    for s in range(last):
        plan((s + 1) * hops + 1, functools.partial(mine, s))

    def middle():
        for j in range(early, chunks - 1):
            have_late(j)
            for s in range(last):
                late(j, s)

    plan(last * hops + 2, middle)

    forwarded = 0
    for s in range(pieces):
        cross(s).wait_recv()
        for way, (exists, _) in enumerate(ways):
            @pl.when(exists)
            def _(way=way):
                lift(s, 1, way).start()
        give(s, line, 1).start()
        for i in range(hops):
            if i == hops - 1 and s + 2 < pieces:
                start_own(s + 2)
            for rel in range(2):
                relay(s, i, rel).wait_recv()

                @pl.when(others[i][1])
                def _():
                    relay(s, i, rel).start()

                give(s, others[i][0], rel).start()
            point = s * hops + i + 1
            flush()
            for j in forwards.get(point, []):
                beside(j).wait_recv()
                for n in range(bands - 1):
                    hand(n, j).start()
                forwarded += 1
                feed(len(order) if forwarded == chunks else 4 + 3 * forwarded)
                if forwarded == chunks:
                    feed(len(order))
                    for k in range(early, chunks):
                        for n in range(bands - 1):
                            spread(n, k).start()
            for job in work.get(point, []):
                job()
                if s == last and i == 0:
                    flush()
            if s == last:
                if i == 0:
                    partial(-1)
                partial(i)

    settle(last)
    have_all(last)
    for j in range(early, chunks - 1):
        have_late(j)
        late(j, last)
    flush()
    sweep(side, 0, chunks + early, total, cols(last), last)
    for j in range(max(early, chunks - 1), chunks):
        have_late(j)
        for s in range(last):
            late(j, s)
    for j in range(max(early, chunks - 1), chunks):
        late(j, last)
    for s in range(pieces):
        out_ref[:, :, quarter(side, s)] = total[:, :, cols(s)].astype(out_ref.dtype)

    for s in range(pieces):
        back(s).wait_recv()
        back(s).wait_send()
        cross(s).wait_send()
        give(s, line, 1).wait_send()
        for rel in range(2):
            for way, (exists, _) in enumerate(ways):
                @pl.when(exists)
                def _(way=way):
                    lift(s, rel, way).wait_send()
        for i in range(hops):
            for rel in range(2):
                @pl.when(others[i][1])
                def _():
                    relay(s, i, rel).wait_send()

                give(s, others[i][0], rel).wait_send()
    mate.wait_send()
    for j in range(chunks):
        beside(j).wait_send()
        for n in range(bands - 1):
            spread(n, j).wait_send()
            hand(n, j).wait_send()


def cuts_of(share):
    cuts = []
    at = 0
    while at < share:
        size = TILE if share - at > TILE else min(LANES, share - at)
        cuts.append((at, size))
        at += size
    return cuts


def solution(mesh):
    bands, rows = mesh.shape["band"], mesh.shape["row"]
    lines = rows // (SIDES * CORES)

    def body(coeffs, rotation):
        height, width = coeffs.shape[1:]
        depth, columns = rotation.shape[1:]
        share = columns // SIDES
        cuts = cuts_of(share)
        pieces = len(cuts)
        chunk = min(CHUNK, width)
        chunks = width // chunk
        dma = pltpu.SemaphoreType.DMA
        return pl.pallas_call(
            functools.partial(kernel, lines, bands, cuts, chunk),
            out_shape=pltpu.VMEM(coeffs.shape, jnp.bfloat16),
            in_specs=[pl.BlockSpec(memory_space=pl.ANY)] * 2,
            out_specs=pl.BlockSpec(memory_space=pltpu.VMEM),
            scratch_shapes=[
                pltpu.VMEM((2, rows * depth, share), jnp.bfloat16),
                pltpu.VMEM((SIDES, bands, 2, height, width), jnp.bfloat16),
                pltpu.VMEM((2, height, share), jnp.float32),
                pltpu.VMEM((2, height, TILE), jnp.float32),
                pltpu.VMEM((2, height, share), jnp.bfloat16),
                dma((2,)),
                dma((pieces,)),
                dma((pieces,)),
                dma((pieces, 2, 2)),
                dma((pieces, lines - 1, 2)),
                dma((pieces, lines, 2)),
                dma((1,)),
                dma((1,)),
                dma((pieces, lines, 2)),
                dma((pieces, lines, 2)),
                dma((chunks,)),
                dma((chunks,)),
                dma((bands - 1, chunks)),
                dma((bands - 1, chunks)),
                dma((bands - 1, chunks)),
                dma((bands - 1, chunks)),
                dma((pieces,)),
                dma((pieces,)),
            ],
            compiler_params=pltpu.CompilerParams(
                collective_id=0, has_side_effects=True, vmem_limit_bytes=54 * 1024 * 1024
            ),
        )(coeffs, rotation)

    in_specs = (P(None, "row", "band"), P(None, "row", "band"))
    out_specs = P(None, "row", "band")
    return jax.shard_map(body, mesh=mesh, in_specs=in_specs, out_specs=out_specs, check_vma=False)
```

time: 169 us -> 180 us (1.065)
  Pallas kernels: 166 us -> 178 us
    pallas_call x1, Pallas kernels: 166 us -> 178 us  [body(): pl.pallas_call(functools.partial(kernel, lines, bands, cuts, chunk), out_...]
where the time goes in v1:
time: 180 us
  Pallas kernels  178 us (99%)
    pallas_call x1, Pallas kernels, body(): pl.pallas_call(functools.partial(kernel, lines, bands, cuts, chunk), out_...  178 us

profile of v1, /device:TPU:25, one launch (start us, length us, event | category | flops | bytes accessed | tf_op | source)
XLA Modules:
  0.0 180.1 jit_solution(1135956231606300922)
XLA Ops:
  0.0 178.4 %shard_map.28 = bf16[2,384,2048]{2,1,0:T(8,128)(2,1)S(1)} custom-call(bf16[2,384,2048]{2,1,0:T(8,128)(2,1)} %coeffs_ref.1, bf16[2,256,2048]{2,1,0:T(8,128)(2,1)} %rotation_ref.1), custom_call_target="tpu_custom_call" | custom-call | tf_op jit(solution)/shard_map/pallas_call | solution.py:382
  178.4 1.7 copy.4

commit v2 on v1

--- a/solution.py
+++ b/solution.py
@@ -13,10 +13,23 @@
 CHUNK = 512
 LANES = 128
 TILE = 256
-FORWARDS = (2, 4, 5, 8)
-
-
-def kernel(lines, bands, cuts, chunk, coeffs_ref, rotation_ref, out_ref, held, whole, total, extra, staged,
+
+FORWARDS = ((0, 2, 1), (1, 1, 1), (1, 2, 1), (2, 1, 1))
+
+JOBS = {
+    (1, 1, 1): ((0, 0, 6, 0, 1, False), (1, 0, 2, 0, 1, False)),
+    (2, 1, 1): ((0, 0, 6, 1, 2, False),),
+    (2, 2, 0): ((1, 0, 2, 1, 2, False), (1, 2, 4, 0, 2, False)),
+    (2, 2, 1): ((1, 4, 6, 0, 2, False),),
+    (3, 1, 0): ((1, 6, 8, 0, 2, True), (1, 0, 8, 2, 3, True)),
+    (3, 3, 0): ((0, 0, 6, 2, 3, False),),
+    (4, 1, 0): ((1, 0, 8, 3, 4, True),),
+    (4, 1, 1): ((0, 0, 6, 3, 4, False),),
+    (4, 2, 0): ((0, 6, 7, 0, 4, False),),
+}
+
+
+def kernel(lines, bands, cuts, chunk, coeffs_ref, rotation_ref, out_ref, held, whole, total, staged,
            own_sem, cross_send, cross_recv, line_send, relay_send, line_recv, mate_send, mate_recv,
            pair_send, pair_recv, side_send, side_recv, band_send, band_recv, pass_send, pass_recv,
            out_send, out_recv):
@@ -162,174 +175,165 @@
         copy.start()
     total[...] = jnp.zeros_like(total)
 
-    def unit(x, start, size, target, to, s):
+    every = bands * chunks
+    pair = 2 if chunks % 2 == 0 else 1
+    ready = set()
+    left = {(rel, s): set(range(every)) for rel in range(2) for s in range(pieces)}
+
+    def once(key, waits):
+        if key not in ready:
+            ready.add(key)
+            for copy, action in waits():
+                getattr(copy, action)()
+
+    def have_coeffs(rel, u):
+        n, j = u // chunks, u % chunks
+        if n == 0 and rel == 0:
+            once("own", lambda: [(own[1], "wait")])
+        elif rel == 0:
+            once((0, u), lambda: [(spread(n - 1, j), "wait_recv")])
+        elif n > 0:
+            once((1, u), lambda: [(hand(n - 1, j), "wait_recv")])
+
+    def have_layer(s, i):
+        if i < 0:
+            once("mate", lambda: [(mate, "wait_recv"), (own[0], "wait")])
+            once((s, i, "layer"), lambda: [(give(s, line, 1), "wait_recv")])
+        else:
+            once((s, i, "layer"), lambda: [(give(s, others[i][0], rel), "wait_recv") for rel in range(2)])
+
+    def unit(rel, start, size, to):
+        x = (side, 1 - side)[rel]
         which = start // width
         at_k = pl.ds(pl.multiple_of(start % width, LANES), size)
         deep = pl.ds(pl.multiple_of(start, LANES), size)
-        real, imag = held[0, deep, cols(s)], held[1, deep, cols(s)]
+        real, imag = held[0, deep, to], held[1, deep, to]
         dot = functools.partial(jnp.dot, preferred_element_type=jnp.float32)
         left_real = whole[x, which, 0, :, at_k]
         left_imag = whole[x, which, 1, :, at_k]
-        target[0, :, to] += dot(left_real, real) - dot(left_imag, imag)
-        target[1, :, to] += dot(left_imag, real) + dot(left_real, imag)
-
-    every = bands * chunks
-    pair = 2 if chunks % 4 == 0 else 1
-
-    def sweep(x, first, stop, target, to, s):
-        @pl.loop(first // pair, stop // pair)
-        def _(u):
-            unit(x, ((band * chunks + u * pair) % every) * chunk, pair * chunk, target, to, s)
-
-    ready = set()
-
-    def once(key, waits):
-        if key not in ready:
-            ready.add(key)
-            for wait in waits():
-                wait()
-
-    def have_mate():
-        once("mate", lambda: [mate.wait_recv, own[0].wait])
-
-    def have_own():
-        once("own", lambda: [own[1].wait] + [spread(n, j).wait_recv for n in range(bands - 1) for j in range(early)])
-
-    def have_layer(s, i):
-        if i < 0:
-            have_mate()
-            once((s, i), lambda: [give(s, line, 1).wait_recv])
-        else:
-            once((s, i), lambda: [give(s, others[i][0], rel).wait_recv for rel in range(2)])
-
-    def have_all(s):
-        for i in range(-1, hops):
-            have_layer(s, i)
-
-    def have_side():
-        once("pass", lambda: [hand(n, j).wait_recv for n in range(bands - 1) for j in range(chunks)])
-
-    def have_late(j):
-        once(("late", j), lambda: [spread(n, j).wait_recv for n in range(bands - 1)])
+        total[rel, 0, :, to] += dot(left_real, real) - dot(left_imag, imag)
+        total[rel, 1, :, to] += dot(left_imag, real) + dot(left_real, imag)
+
+    def sweep(rel, low, high, first, stop):
+        for s in range(first, stop):
+            for i in range(-1, hops):
+                have_layer(s, i)
+            left[rel, s] -= set(range(low, high))
+        for u in range(low, high):
+            have_coeffs(rel, u)
+        step = pair if low % pair == 0 and high % pair == 0 else 1
+        count = (high - low) // step
+        at, size = cuts[first]
+
+        @pl.loop(0, count * (stop - first))
+        def _(t):
+            u = low + t % count * step
+            to = pl.ds(pl.multiple_of(at + t // count * size, LANES), size)
+            unit(rel, (band * chunks + u) % every * chunk, step * chunk, to)
+
+    def finish(rel, s):
+        run = sorted(left[rel, s])
+        while run:
+            n = 1
+            while n < len(run) and run[n] == run[0] + n:
+                n += 1
+            sweep(rel, run[0], run[0] + n, s, s + 1)
+            run = run[n:]
 
     pending = []
 
     def flush():
         while pending:
-            back(pending.pop()).start()
+            back(pending.pop(0)).start()
 
     def settle(s):
-        staged[:, :, cols(s)] = extra[:, :, pl.ds(0, cuts[s][1])].astype(staged.dtype)
+        staged[:, :, cols(s)] = total[1, :, :, cols(s)].astype(staged.dtype)
         pending.append(s)
 
-    def mine(s):
-        have_own()
-        have_all(s)
-        sweep(side, 0, chunks + early, total, cols(s), s)
-
-    def theirs(s):
-        have_own()
-        have_side()
-        have_all(s)
-        to = pl.ds(0, cuts[s][1])
-        extra[:, :, to] = jnp.zeros((2, extra.shape[1], cuts[s][1]), extra.dtype)
-        sweep(1 - side, 0, every, extra, to, s)
-        settle(s)
-
     def partial(i):
-        have_own()
-        have_side()
+        for u in range(every):
+            have_coeffs(1, u)
         have_layer(last, i)
-        z = line if i < 0 else others[i][0]
-        to = pl.ds(0, cuts[last][1])
-        if i < 0:
-            extra[:, :, to] = jnp.zeros((2, extra.shape[1], cuts[last][1]), extra.dtype)
-        unit(1 - side, z * layer, layer, extra, to, last)
-
-    def late(j, s):
-        for n in range(1, bands):
-            if n > 1 or j >= early:
-                unit(side, ((band + n) % bands) * width + j * chunk, chunk, total, cols(s), s)
-
-    work = {}
-
-    def plan(point, job):
-        work.setdefault(min(point, pieces * hops), []).append(job)
-
-    forwards = {}
-    for j in range(chunks):
-        hint = FORWARDS[j] if j < len(FORWARDS) else FORWARDS[-1]
-        forwards.setdefault(min(hint, pieces * hops), []).append(j)
-    begin = max(0, (pieces - 2) * hops + 1)
-    for s in range(last):
-        plan(max((s + 1) * hops + 1, begin + s), functools.partial(theirs, s))
-    for s in range(last):
-        plan((s + 1) * hops + 1, functools.partial(mine, s))
-
-    def middle():
-        for j in range(early, chunks - 1):
-            have_late(j)
-            for s in range(last):
-                late(j, s)
-
-    plan(last * hops + 2, middle)
-
-    forwarded = 0
-    for s in range(pieces):
+        unit(1, (line if i < 0 else others[i][0]) * layer, layer, cols(last))
+
+    def work(job):
+        rel, low, high, first, stop, settled = job
+        stop = min(stop, last + 1 - rel)
+        high = min(high, every)
+        while first < stop:
+            end = first
+            while end < stop and cuts[end][1] == cuts[first][1]:
+                end += 1
+            if set(range(low, high)) <= left[rel, first] and low < high:
+                sweep(rel, low, high, first, end)
+            if settled:
+                for s in range(first, end):
+                    finish(rel, s)
+                    settle(s)
+            first = end
+
+    def enter(s):
         cross(s).wait_recv()
         for way, (exists, _) in enumerate(ways):
             @pl.when(exists)
             def _(way=way):
                 lift(s, 1, way).start()
         give(s, line, 1).start()
+
+    def arrive(s, i, rel):
+        if i == hops - 1 and rel == 0 and s + 2 < pieces:
+            start_own(s + 2)
+        relay(s, i, rel).wait_recv()
+
+        @pl.when(others[i][1])
+        def _():
+            relay(s, i, rel).start()
+
+        give(s, others[i][0], rel).start()
+
+    forwarded = 0
+    for s in range(pieces):
         for i in range(hops):
-            if i == hops - 1 and s + 2 < pieces:
-                start_own(s + 2)
             for rel in range(2):
-                relay(s, i, rel).wait_recv()
-
-                @pl.when(others[i][1])
-                def _():
-                    relay(s, i, rel).start()
-
-                give(s, others[i][0], rel).start()
-            point = s * hops + i + 1
-            flush()
-            for j in forwards.get(point, []):
-                beside(j).wait_recv()
-                for n in range(bands - 1):
-                    hand(n, j).start()
-                forwarded += 1
-                feed(len(order) if forwarded == chunks else 4 + 3 * forwarded)
-                if forwarded == chunks:
-                    feed(len(order))
-                    for k in range(early, chunks):
-                        for n in range(bands - 1):
-                            spread(n, k).start()
-            for job in work.get(point, []):
-                job()
-                if s == last and i == 0:
-                    flush()
+                point = (s, i + 1, rel)
+                if i == 0 and rel == 0:
+                    enter(s)
+                arrive(s, i, rel)
+                flush()
+                while forwarded < chunks and (FORWARDS[min(forwarded, len(FORWARDS) - 1)] <= point or s == last):
+                    j = forwarded
+                    beside(j).wait_recv()
+                    for n in range(bands - 1):
+                        hand(n, j).start()
+                    forwarded += 1
+                    feed(4 + 3 * forwarded)
+                    if forwarded == chunks:
+                        feed(len(order))
+                        for k in range(early, chunks):
+                            for n in range(bands - 1):
+                                spread(n, k).start()
+                for job in JOBS.get(point, ()):
+                    work(job)
             if s == last:
                 if i == 0:
+                    for t in range(last):
+                        if left[1, t]:
+                            finish(1, t)
+                            settle(t)
                     partial(-1)
-                partial(i)
+
+    for i in range(hops):
+        partial(i)
 
     settle(last)
-    have_all(last)
-    for j in range(early, chunks - 1):
-        have_late(j)
-        late(j, last)
+    if set(range(pair)) <= left[0, last]:
+        sweep(0, 0, pair, last, pieces)
     flush()
-    sweep(side, 0, chunks + early, total, cols(last), last)
-    for j in range(max(early, chunks - 1), chunks):
-        have_late(j)
-        for s in range(last):
-            late(j, s)
-    for j in range(max(early, chunks - 1), chunks):
-        late(j, last)
-    for s in range(pieces):
-        out_ref[:, :, quarter(side, s)] = total[:, :, cols(s)].astype(out_ref.dtype)
+    finish(0, last)
+    work((0, every - 1, every, 0, last, False))
+    for s in range(last):
+        finish(0, s)
+    out_ref[:, :, half(side)] = total[0].astype(out_ref.dtype)
 
     for s in range(pieces):
         back(s).wait_recv()
@@ -387,8 +391,7 @@
             scratch_shapes=[
                 pltpu.VMEM((2, rows * depth, share), jnp.bfloat16),
                 pltpu.VMEM((SIDES, bands, 2, height, width), jnp.bfloat16),
-                pltpu.VMEM((2, height, share), jnp.float32),
-                pltpu.VMEM((2, height, TILE), jnp.float32),
+                pltpu.VMEM((2, 2, height, share), jnp.float32),
                 pltpu.VMEM((2, height, share), jnp.bfloat16),
                 dma((2,)),
                 dma((pieces,)),

time: 180 us -> 166 us (0.922)
  Pallas kernels: 178 us -> 163 us
    pallas_call x1, Pallas kernels: 178 us -> 163 us  [body(): pl.pallas_call(functools.partial(kernel, lines, bands, cuts, chunk), out_...]
where the time goes in v2:
time: 166 us; the launch traced here: 164 us
  Pallas kernels  163 us (98%)
  local copies, waits for them, and re-layouts  1.67 us (1%)
    pallas_call x1, Pallas kernels, body(): pl.pallas_call(functools.partial(kernel, lines, bands, cuts, chunk), out_...  163 us

profile of v2, /device:TPU:25, one launch (start us, length us, event | category | flops | bytes accessed | tf_op | source)
XLA Modules:
  0.0 164.5 jit_solution(11786893168274885214)
XLA Ops:
  0.0 162.8 %shard_map.28 = bf16[2,384,2048]{2,1,0:T(8,128)(2,1)S(1)} custom-call(bf16[2,384,2048]{2,1,0:T(8,128)(2,1)} %coeffs_ref.1, bf16[2,256,2048]{2,1,0:T(8,128)(2,1)} %rotation_ref.1), custom_call_target="tpu_custom_call" | custom-call | tf_op jit(solution)/shard_map/pallas_call | solution.py:386
  162.8 1.7 %copy.4 = bf16[2,384,2048]{2,1,0:T(8,128)(2,1)} copy(bf16[2,384,2048]{2,1,0:T(8,128)(2,1)S(1)} %shard_map.28) | data formatting | bytes 6291456
